TPU v7x, 128 devices: a whole 4x4x4 slice. The times are simulated.
128 devices in a mesh: leaf: 32 (over z, y, core), probe: 4 (over x).
Axes of the slice: x: 4, y: 4, z: 4, core: 2. Of those that a mesh axis runs over, the one named last changes fastest.
Arguments:
- coords: float32 [3, 131072], P(None, 'leaf'), may hold values from 0 to 1
- weights: float32 [131072], P('leaf'), may hold values from 0.01 to 0.1
- omega: bfloat16 [256, 131072], P('probe', 'leaf'), may hold values from -6 to 6
- near_local: int32 [1024, 24], P('leaf'), may hold values from 0 to 1023, as said below
- far_pairs: int32 [2, 8192], P(None, 'leaf'), may hold values from 0 to 1023, as said below
- skel_rows: int32 [1024, 32], P('leaf'), may hold values from 0 to 127, as said below
- parent_interp: bfloat16 [128, 256, 64], P('leaf'), may hold values from -0.375 to 0.375
Outputs:
- near_sample: float32 [256, 131072], P('probe', 'leaf')
- parent_sample: float32 [256, 8192], P('probe', 'leaf')
Inputs may be any that keep to these rules, and one draw needn't show every extreme that they name: `near_local`: entry 0 of leaf t's row is t itself; every other entry names a leaf of the same device as t (equal index // 32); repeats may occur. `far_pairs`: column c belongs to device c // 256: its source leaf lies on that device and its target leaf on another device. Of one device's 256 columns at most 16 have targets on any one other device, and one device receives exactly 16 from every other device. `skel_rows`: the 32 numbers of one leaf are distinct.
All inputs are finite; a program needn't handle non-finite values.
Results may differ from a plain program's by a relative error of at most 0.008.
Values may be sent and summed in bfloat16 or wider, within the bound.
A program may use at most 64 MiB of HBM per device.

v0:
```python
import jax
import jax.numpy as jnp
from jax import lax
from jax.experimental import pallas as pl
from jax.experimental.pallas import tpu as pltpu
from jax.sharding import PartitionSpec as P

PTS = 128
SK = 32
SK2 = 64
CHILD = 8
CAP = 16
LEAF_DEV = 32
RING = 16
NSUB = 4
JSTEP = 512
DELTA_SQ = 0.0001
INV_FOUR_PI = 0.07957747154594767

VMEM = pl.BlockSpec(memory_space=pltpu.VMEM)
SMEM = pl.BlockSpec(memory_space=pltpu.SMEM)
ANY = pl.BlockSpec(memory_space=pl.ANY)
MESH = pl.DeviceIdType.MESH
BF = jnp.bfloat16
F32 = jnp.float32
I32 = jnp.int32


def ring_position(leaf):
    z, y, core = leaf // 8, (leaf // 2) % 4, leaf % 2
    return 4 * (y * (1 - core) + z * core) + (y + z) % 4


def ring_device(core, position):
    p = (position + 2 * RING) % RING
    r, c = p // 4, p % 4
    o = (c - r + 4) % 4
    y = r * (1 - core) + o * core
    z = o * (1 - core) + r * core
    return (z * 4 + y) * 2 + core


def split3(v):
    a = v.astype(BF).astype(F32)
    b = (v - a).astype(BF).astype(F32)
    c = (v - a - b).astype(BF).astype(F32)
    return a, b, c


def kernel_body(
    om_ref, coords_ref, w_ref, near_ids_ref, far_pairs_ref, skel_ref, interp_ref, near_ref, parent_ref, *s
):
    bufs, pbufs = list(s[:16]), list(s[16:32])
    mb, pmb = list(s[32:48]), list(s[48:64])
    tb, ptb = list(s[64:80]), list(s[80:96])
    (om_flat, rec, last, tile, srec, slast, fx, fy, cntx, xb, chain, et, merged, energy, got,
     ssem, rsem, pssem, prsem, xssem, xrsem, csem, lsem, essem, ersem) = s[96:]
    me = lax.axis_index("leaf")
    x = lax.axis_index("probe")
    n_probe = lax.axis_size("probe")
    core = me % 2
    pos = ring_position(me)
    nxt, prv = ring_device(core, pos + 1), ring_device(core, pos - 1)
    partner = me + 1 - 2 * core
    rows, n = om_ref.shape
    per_sub = LEAF_DEV // NSUB
    per_probe = LEAF_DEV // n_probe
    barrier = pltpu.get_barrier_semaphore()
    for dev in (nxt, prv, partner):
        pl.semaphore_signal(barrier, inc=1, device_id=(dev, x), device_id_type=MESH)
    for k in range(1, n_probe):
        pl.semaphore_signal(barrier, inc=1, device_id=(me, (x + k) % n_probe), device_id_type=MESH)
    for t in range(LEAF_DEV):
        sl = slice(t * PTS, (t + 1) * PTS)
        v = (om_ref[:, sl].astype(F32) * (w_ref[:, sl] * INV_FOUR_PI)).astype(BF)
        bufs[0][t] = v
        om_flat[:, sl] = v
        mb[0][t] = coords_ref[:, sl]
    pl.semaphore_wait(barrier, 3 + n_probe - 1)

    def remote(src, dst, ss, rs, dev, probe=None):
        return pltpu.make_async_remote_copy(
            src_ref=src, dst_ref=dst, send_sem=ss, recv_sem=rs,
            device_id=(dev, x if probe is None else probe), device_id_type=MESH,
        )

    def ends(d, way):
        return (d, d + 1, nxt) if way == 0 else ((RING - d) % RING, RING - d - 1, prv)

    def ring_om(d, sub, way):
        i, j, dev = ends(d, way)
        sl = pl.ds(sub * per_sub, per_sub)
        return remote(bufs[i].at[sl], bufs[j].at[sl], ssem.at[way, d, sub], rsem.at[way, d, sub], dev)

    def ring_pts(d, way):
        i, j, dev = ends(d, way)
        sl = pl.ds(x * per_probe, per_probe)
        return remote(mb[i].at[sl], mb[j].at[sl], ssem.at[way, d, NSUB], rsem.at[way, d, NSUB], dev)

    def probe_pts(i, k):
        sl = pl.ds(x * per_probe, per_probe)
        return remote(mb[i].at[sl], mb[i].at[sl], xssem.at[i, k - 1], xrsem.at[i, k - 1], me, (x + k) % n_probe)

    def probe_pts_in(i, k):
        sl = pl.ds(((x + n_probe - k) % n_probe) * per_probe, per_probe)
        return remote(mb[i].at[sl], mb[i].at[sl], xssem.at[i, k - 1], xrsem.at[i, k - 1], me, (x + k) % n_probe)

    def ring_tab(d, way):
        i, j, dev = ends(d, way)
        return remote(tb[i], tb[j], ssem.at[way, d, NSUB + 1], rsem.at[way, d, NSUB + 1], dev)

    def pair_om(i, sub):
        sl = pl.ds(sub * per_sub, per_sub)
        return remote(bufs[i].at[sl], pbufs[i].at[sl], pssem.at[i, sub], prsem.at[i, sub], partner)

    def pair_pts(i):
        return remote(mb[i], pmb[i], pssem.at[i, NSUB], prsem.at[i, NSUB], partner)

    def pair_tab(i):
        return remote(tb[i], ptb[i], pssem.at[i, NSUB + 1], prsem.at[i, NSUB + 1], partner)

    def subs(d, way):
        if d < 7:
            return range(NSUB)
        return range(NSUB // 2) if way == 0 else range(NSUB // 2, NSUB)

    def small(d, way):
        return d < 7 or way == 0

    def make_table():
        def column(row):
            return jnp.concatenate(
                [jnp.broadcast_to(row[:, h * PTS:(h + 1) * PTS], (PTS, PTS)).T for h in range(row.shape[1] // PTS)], axis=0
            )

        src = lax.bitwise_and(far_pairs_ref[0:1, :], LEAF_DEV - 1)
        tgt = far_pairs_ref[1:2, :]
        m = tgt.shape[1]
        tcol = column(tgt)
        rank = []
        for h in range(m // PTS):
            trow = jnp.broadcast_to(tgt[:, h * PTS:(h + 1) * PTS], (m, PTS))
            sub_i = lax.broadcasted_iota(I32, (m, PTS), 0)
            lane_i = lax.broadcasted_iota(I32, (m, PTS), 1) + h * PTS
            same = lax.shift_right_logical(trow, 5) == lax.shift_right_logical(tcol, 5)
            before = (tcol < trow) | ((tcol == trow) & (sub_i < lane_i))
            rank.append(jnp.sum((same & before).astype(I32), axis=0, keepdims=True))
        rank = jnp.concatenate(rank, axis=1)
        slot = column(lax.shift_right_logical(tgt, 5) * CAP + rank)
        code = column(src * LEAF_DEV + lax.bitwise_and(tgt, LEAF_DEV - 1) + 1)
        lane_i = lax.broadcasted_iota(I32, (m, PTS), 1)
        for r in range(tb[0].shape[0]):
            hit = slot == lane_i + r * PTS
            tb[0][r:r + 1, :] = jnp.sum(jnp.where(hit, code, 0), axis=0, keepdims=True) - 1

    def link(c, tab):
        row = tab[pl.ds(me // 8, 1), :]
        tile[...] = jnp.broadcast_to(row, (PTS, PTS)).T
        code = tile[pl.ds((me % 8) * CAP, CAP), :]
        sub_i = lax.broadcasted_iota(I32, (CAP, PTS), 0)
        lane_i = lax.broadcasted_iota(I32, (CAP, PTS), 1)
        valid = code >= 0
        target = jnp.where(valid, lax.bitwise_and(code, LEAF_DEV - 1), PTS)
        hit = target == lane_i
        run = valid & (sub_i > 0) & (target == pltpu.roll(target, 1, 0))
        prev = jnp.sum(jnp.where(hit, jnp.broadcast_to(last[...], (CAP, PTS)), 0), axis=1, keepdims=True)
        prev = jnp.where(run, 0, prev)
        word = jnp.where(valid, code, 0) + prev * 1024 + run.astype(I32) * (1024 * 1024)
        rec[c] = jnp.sum(jnp.where(sub_i == lane_i, word, 0), axis=0, keepdims=True)
        new = jnp.max(jnp.where(hit, sub_i + c * CAP, 0), axis=0, keepdims=True)
        last[...] = jnp.where(new > 0, new, last[...])

    def link_out(c):
        return pltpu.make_async_copy(rec.at[c], srec.at[c], csem.at[c])

    def far_chunk(c, om, pts):
        def body(b, full):
            for u in range(8):
                k = b * 8 + u
                word = srec[c, 0, k]
                src = lax.bitwise_and(lax.shift_right_logical(word, 5), LEAF_DEV - 1)
                t = lax.bitwise_and(word, LEAF_DEV - 1)
                prev = lax.bitwise_and(lax.shift_right_logical(word, 10), 1023)
                run = lax.shift_right_logical(word, 20).astype(F32)
                p = pts[src]
                dist = None
                for d in range(3):
                    dx = xb[t, d] - p[d:d + 1]
                    dist = dx * dx if dist is None else dist + dx * dx
                kern = lax.rsqrt((dist + DELTA_SQ).astype(BF))
                r = lax.dot_general(om[src], kern, (((1,), (1,)), ((), ())), preferred_element_type=F32)
                full = r + chain[prev] + full * run
                chain[c * CAP + k] = full
            return full

        lax.fori_loop(0, CAP // 8, body, jnp.zeros((rows, PTS), F32))

    def prepare():
        lane8 = lax.broadcasted_iota(I32, (8, PTS), 0)

        def leaf(t, carry):
            sl = pl.ds(pl.multiple_of(t * PTS, PTS), PTS)
            raw = mb[0][t]
            for d in range(3):
                xb[t, d] = jnp.broadcast_to(raw[d:d + 1], (PTS, PTS)).T
            c = raw - 0.5
            cx, cy, cz = c[0:1], c[1:2], c[2:3]
            q = cx * cx + cy * cy + cz * cz

            def stack(r0, r1, r2, r3, r4):
                v = jnp.where(lane8 == 0, r0, 0.0)
                v = jnp.where(lane8 == 1, r1, v)
                v = jnp.where(lane8 == 2, r2, v)
                v = jnp.where(lane8 == 3, r3, v)
                return jnp.where(lane8 == 4, r4, v)

            a1, a2, a3 = split3(stack(cx, cy, cz, q, 1.0))
            b1, b2, b3 = split3(stack(-2.0 * cx, -2.0 * cy, -2.0 * cz, 1.0, q + DELTA_SQ))
            left = jnp.concatenate([a1, a1, a2, a2, a1, a3], axis=0)
            fx[sl, :] = left.T.astype(BF)
            fy[:, sl] = jnp.concatenate([b1, b2, b1, b2, b3, b1], axis=0).astype(BF)
            return carry

        lax.fori_loop(0, LEAF_DEV, leaf, 0)
        ids = near_ids_ref[...] - me * LEAF_DEV
        sub_i = lax.broadcasted_iota(I32, (LEAF_DEV, LEAF_DEV), 0)
        cnt = jnp.zeros((LEAF_DEV, LEAF_DEV), F32)
        for e in range(ids.shape[0]):
            cnt = cnt + (ids[e:e + 1, :] == sub_i).astype(F32)
        cnt = cnt.T
        for t in range(LEAF_DEV):
            cntx[:, t * PTS:(t + 1) * PTS] = jnp.broadcast_to(cnt[:, t:t + 1], (LEAF_DEV, PTS))

    def prepare_merge():
        for t in range(LEAF_DEV):
            pick = (lax.broadcasted_iota(I32, (PTS, SK), 0) == skel_ref[t:t + 1, :]).astype(F32).astype(BF)
            part = interp_ref[t // CHILD, :, (t % CHILD) * SK:(t % CHILD + 1) * SK]
            et[t] = lax.dot_general(part, pick, (((1,), (1,)), ((), ())), preferred_element_type=F32).astype(BF)

    def near_part(strip, half):
        here = pl.ds(pl.multiple_of(strip * 256, 256), 256)
        acc = None
        for j in range(half * n // 2, (half + 1) * n // 2, JSTEP):
            d = jnp.dot(fx[here, :], fy[:, j:j + JSTEP], preferred_element_type=F32)
            k = lax.rsqrt(d.astype(BF))
            c0 = cntx[pl.ds(2 * strip, 1), j:j + JSTEP].astype(BF)
            c1 = cntx[pl.ds(2 * strip + 1, 1), j:j + JSTEP].astype(BF)
            k = jnp.concatenate([k[:PTS] * c0, k[PTS:] * c1], axis=0)
            r = lax.dot_general(om_flat[:, j:j + JSTEP], k, (((1,), (1,)), ((), ())), preferred_element_type=F32)
            acc = r if acc is None else acc + r
        if half == 0:
            near_ref[:, here] = acc
        else:
            near_ref[:, here] += acc

    near_work = [(st, h) for st in range(LEAF_DEV // 2) for h in range(2)]
    far_ready = []

    def do_near(m):
        for a, b in near_work[:m]:
            near_part(a, b)
        del near_work[:m]

    def do_far(m):
        for _ in range(min(m, len(far_ready))):
            kind, i = far_ready.pop(0)
            c = i + kind * RING
            if kind:
                for sub in range(NSUB):
                    pair_om(i, sub).wait_recv()
                pair_pts(i).wait_recv()
            link_out(c).wait()
            far_chunk(c, (pbufs if kind else bufs)[i], (pmb if kind else mb)[i])

    for way in (0, 1):
        ring_pts(0, way).start()
        ring_om(0, 0, way).start()
    make_table()
    for sub in range(1, NSUB):
        for way in (0, 1):
            ring_om(0, sub, way).start()
    pair_pts(0).start()
    for sub in range(NSUB):
        pair_om(0, sub).start()
    last[...] = jnp.zeros((1, PTS), I32)
    chain[0] = jnp.zeros((rows, PTS), F32)
    prepare()
    for way in (0, 1):
        ring_tab(0, way).start()
    pair_tab(0).start()
    do_near(1)

    def links(chunks):
        for kind, i in chunks:
            if kind:
                pair_tab(i).wait_recv()
            link(i + kind * RING, (ptb if kind else tb)[i])
        return chunks

    for d in range(8):
        ways = [way for way in (0, 1) if small(d, way)]
        for way in ways:
            i = ends(d, way)[1]
            ring_pts(d, way).wait_recv()
            if d < 7 and small(d + 1, way):
                ring_pts(d + 1, way).start()
            for k in range(1, n_probe):
                probe_pts(i, k).start()

        def tables():
            for way in ways:
                i = ends(d, way)[1]
                ring_tab(d, way).wait_recv()
                if d < 7 and small(d + 1, way):
                    ring_tab(d + 1, way).start()
                pair_tab(i).start()

        def points():
            for way in ways:
                i = ends(d, way)[1]
                for k in range(1, n_probe):
                    probe_pts_in(i, k).wait_recv()
                pair_pts(i).start()

        arrived = [(kind, ends(d, way)[1]) for kind in (0, 1) for way in ways]
        if d == 0:
            arrived = [(1, 0)] + arrived
        for sub in range(NSUB):
            for way in (0, 1):
                if sub not in subs(d, way):
                    continue
                i = ends(d, way)[1]
                ring_om(d, sub, way).wait_recv()
                if d < 7 and sub in subs(d + 1, way):
                    ring_om(d + 1, sub, way).start()
                pair_om(i, sub).start()
            if sub == 0:
                tables()
            if d < 7:
                do_near(2 if d == 0 else 1)
                do_far(1)
            if sub == 1:
                points()
        if d == 7:
            links(arrived)
            do_far(1)
            for kind, i in arrived:
                link_out(i + kind * RING).start()
            do_far(len(far_ready))
        else:
            links(arrived)
            do_near(1)
            for kind, i in arrived:
                link_out(i + kind * RING).start()
            if d == 0:
                prepare_merge()
        far_ready += arrived
    last_out = pltpu.make_async_copy(last, slast, lsem)
    last_out.start()
    do_near(len(near_work))
    do_far(len(far_ready))
    last_out.wait()

    for p in range(LEAF_DEV // CHILD):
        m = None
        for t in range(p * CHILD, (p + 1) * CHILD):
            sl = slice(t * PTS, (t + 1) * PTS)
            v = near_ref[:, sl] + chain[slast[0, t]]
            near_ref[:, sl] = v
            r = lax.dot_general(v.astype(BF), et[t], (((1,), (1,)), ((), ())), preferred_element_type=F32)
            m = r if m is None else m + r
        merged[p] = m
        energy[p:p + 1] = jnp.broadcast_to(jnp.sum(m * m), (1, PTS))

    for d in range(8):
        for way in (0, 1):
            for sub in subs(d, way):
                ring_om(d, sub, way).wait_send()
            if small(d, way):
                i = ends(d, way)[1]
                ring_tab(d, way).wait_send()
                ring_pts(d, way).wait_send()
                for k in range(1, n_probe):
                    probe_pts(i, k).wait_send()
    copies = [
        remote(energy, got.at[k - 1], essem.at[k - 1], ersem.at[k - 1], me, (x + k) % n_probe) for k in range(1, n_probe)
    ]
    for cp in copies:
        cp.start()
    for i in range(RING):
        for sub in range(NSUB):
            pair_om(i, sub).wait_send()
        pair_tab(i).wait_send()
        pair_pts(i).wait_send()
    for cp in copies:
        cp.wait()
    total = energy[...]
    for k in range(n_probe - 1):
        total = total + got[k]
    factor = lax.rsqrt(total / (SK2 * rows * n_probe) + 1e-06)
    for p in range(LEAF_DEV // CHILD):
        parent_ref[:, p * SK2:(p + 1) * SK2] = merged[p] * factor[p:p + 1, :SK2]


def sample(om, coords, w, near_ids, far_pairs, skel, interp):
    rows, n = om.shape
    n_probe = lax.axis_size("probe")
    parents = LEAF_DEV // CHILD
    slots = 2 * RING * CAP
    dma = pltpu.SemaphoreType.DMA
    return pl.pallas_call(
        kernel_body,
        out_shape=(
            jax.ShapeDtypeStruct((rows, n), F32),
            jax.ShapeDtypeStruct((rows, parents * SK2), F32),
        ),
        in_specs=[VMEM] * 7,
        out_specs=(VMEM, VMEM),
        scratch_shapes=[pltpu.VMEM((LEAF_DEV, rows, PTS), BF)] * 32
        + [pltpu.VMEM((LEAF_DEV, 3, PTS), F32)] * 32
        + [pltpu.VMEM((RING * 2 * CAP // PTS, PTS), I32)] * 32
        + [
            pltpu.VMEM((rows, n), BF),
            pltpu.VMEM((2 * RING, 1, PTS), I32),
            pltpu.VMEM((1, PTS), I32),
            pltpu.VMEM((PTS, PTS), I32),
            pltpu.SMEM((2 * RING, 1, PTS), I32),
            pltpu.SMEM((1, PTS), I32),
            pltpu.VMEM((n, 48), BF),
            pltpu.VMEM((48, n), BF),
            pltpu.VMEM((LEAF_DEV, n), F32),
            pltpu.VMEM((LEAF_DEV, 3, PTS, PTS), F32),
            pltpu.VMEM((slots, rows, PTS), F32),
            pltpu.VMEM((LEAF_DEV, SK2, PTS), BF),
            pltpu.VMEM((parents, rows, SK2), F32),
            pltpu.VMEM((parents, PTS), F32),
            pltpu.VMEM((n_probe - 1, parents, PTS), F32),
            dma((2, 8, NSUB + 2)),
            dma((2, 8, NSUB + 2)),
            dma((RING, NSUB + 2)),
            dma((RING, NSUB + 2)),
            dma((RING, n_probe - 1)),
            dma((RING, n_probe - 1)),
            dma((2 * RING,)),
            dma(()),
            dma((n_probe - 1,)),
            dma((n_probe - 1,)),
        ],
        compiler_params=pltpu.CompilerParams(
            collective_id=0, has_side_effects=True, vmem_limit_bytes=62 * 1024 * 1024
        ),
        name="sample",
    )(om, coords, w, near_ids, far_pairs, skel, interp)


def per_device(coords, weights, omega, near_local, far_pairs, skel_rows, parent_interp):
    return sample(
        omega, coords, weights.reshape(1, -1), near_local.T, far_pairs, skel_rows, parent_interp.transpose(0, 2, 1)
    )


def solution(mesh):
    return jax.shard_map(
        per_device,
        mesh=mesh,
        in_specs=(
            P(None, "leaf"),
            P("leaf"),
            P("probe", "leaf"),
            P("leaf", None),
            P(None, "leaf"),
            P("leaf", None),
            P("leaf", None, None),
        ),
        out_specs=(P("probe", "leaf"), P("probe", "leaf")),
        check_vma=False,
    )
```

profile of v0, /device:TPU:0, one launch (start us, length us, event | category | flops | bytes accessed | tf_op | source)
XLA Modules:
  0.0 91.1 jit_solution(1138140214374529441)
XLA Ops:
  0.6 87.5 %sample.1 = (f32[64,4096]{1,0:T(8,128)}, f32[64,256]{1,0:T(8,128)}) custom-call(bf16[64,4096]{1,0:T(8,128)(2,1)} %om_ref.1, f32[3,4096]{1,0:T(4,128)} %coords_ref.1, f32[1,4096]{1,0:T(1,128)} %bitcast.4, s32[24,32]{1,0:T(8,128)} %bitcast.5, s32[2,256]{1,0:T(2,128)} %far_pairs_ref.1, s32[32,32]{1,0:T(8,128)} %skel_ref.1, bf16[4,64,256]{2,1,0:T(8,128)(2,1)} %bitcast.3), custom_call_target="tpu_custom_call" | custom-call | tf_op jit(solution)/shard_map/sample/pallas_call | solution.py:411
  88.2 0.0 copy-start
  88.2 2.3 %copy.11 = f32[64,4096]{1,0:T(8,128)} copy(f32[64,4096]{1,0:T(8,128)} %get-tuple-element.4) | data formatting | bytes 2097152
  90.5 0.0 copy-done
  90.5 0.6 copy.12
Async XLA Ops:
  88.2 2.3 %copy-start = (f32[64,256]{1,0:T(8,128)S(1)}, f32[64,256]{1,0:T(8,128)}, u32[]{:S(2)}) copy-start(f32[64,256]{1,0:T(8,128)} %get-tuple-element.5) | copy-start | bytes 196612
where the time goes:
time: 91.3 us; the launch traced here: 91.1 us
  Pallas kernels  87.5 us (96%)
  local copies, waits for them, and re-layouts  2.94 us (3%)
    pallas_call x1, Pallas kernels, sample(): pl.pallas_call(kernel_body, out_shape=(jax.ShapeDtypeStruct((rows, n), F3...  87.5 us
    unnamed x4, local copies, waits for them, and re-layouts  2.94 us

commit v1 on v0

--- a/solution.py
+++ b/solution.py
@@ -12,7 +12,7 @@
 CAP = 16
 LEAF_DEV = 32
 RING = 16
-NSUB = 4
+NSUB = 2
 JSTEP = 512
 DELTA_SQ = 0.0001
 INV_FOUR_PI = 0.07957747154594767
@@ -109,9 +109,8 @@
         i, j, dev = ends(d, way)
         return remote(tb[i], tb[j], ssem.at[way, d, NSUB + 1], rsem.at[way, d, NSUB + 1], dev)
 
-    def pair_om(i, sub):
-        sl = pl.ds(sub * per_sub, per_sub)
-        return remote(bufs[i].at[sl], pbufs[i].at[sl], pssem.at[i, sub], prsem.at[i, sub], partner)
+    def pair_om(i):
+        return remote(bufs[i], pbufs[i], pssem.at[i, 0], prsem.at[i, 0], partner)
 
     def pair_pts(i):
         return remote(mb[i], pmb[i], pssem.at[i, NSUB], prsem.at[i, NSUB], partner)
@@ -153,22 +152,30 @@
             hit = slot == lane_i + r * PTS
             tb[0][r:r + 1, :] = jnp.sum(jnp.where(hit, code, 0), axis=0, keepdims=True) - 1
 
-    def link(c, tab):
-        row = tab[pl.ds(me // 8, 1), :]
-        tile[...] = jnp.broadcast_to(row, (PTS, PTS)).T
-        code = tile[pl.ds((me % 8) * CAP, CAP), :]
+    def links(chunks):
+        for h, (kind, i) in enumerate(chunks):
+            if kind:
+                pair_tab(i).wait_recv()
+            row = (ptb if kind else tb)[i][pl.ds(me // 8, 1), :]
+            tile[h] = jnp.broadcast_to(row, (PTS, PTS)).T
         sub_i = lax.broadcasted_iota(I32, (CAP, PTS), 0)
         lane_i = lax.broadcasted_iota(I32, (CAP, PTS), 1)
-        valid = code >= 0
-        target = jnp.where(valid, lax.bitwise_and(code, LEAF_DEV - 1), PTS)
-        hit = target == lane_i
-        run = valid & (sub_i > 0) & (target == pltpu.roll(target, 1, 0))
-        prev = jnp.sum(jnp.where(hit, jnp.broadcast_to(last[...], (CAP, PTS)), 0), axis=1, keepdims=True)
-        prev = jnp.where(run, 0, prev)
-        word = jnp.where(valid, code, 0) + prev * 1024 + run.astype(I32) * (1024 * 1024)
-        rec[c] = jnp.sum(jnp.where(sub_i == lane_i, word, 0), axis=0, keepdims=True)
-        new = jnp.max(jnp.where(hit, sub_i + c * CAP, 0), axis=0, keepdims=True)
-        last[...] = jnp.where(new > 0, new, last[...])
+        newest = last[...]
+        for h, (kind, i) in enumerate(chunks):
+            c = i + kind * RING
+            code = tile[h, pl.ds((me % 8) * CAP, CAP), :]
+            valid = code >= 0
+            target = jnp.where(valid, lax.bitwise_and(code, LEAF_DEV - 1), PTS)
+            hit = target == lane_i
+            run = valid & (sub_i > 0) & (target == pltpu.roll(target, 1, 0))
+            prev = jnp.sum(jnp.where(hit, jnp.broadcast_to(newest, (CAP, PTS)), 0), axis=1, keepdims=True)
+            prev = jnp.where(run, 0, prev)
+            word = jnp.where(valid, code, 0) + prev * 1024 + run.astype(I32) * (1024 * 1024)
+            rec[c] = jnp.sum(jnp.where(sub_i == lane_i, word, 0), axis=0, keepdims=True)
+            new = jnp.max(jnp.where(hit, sub_i + c * CAP, 0), axis=0, keepdims=True)
+            newest = jnp.where(new > 0, new, newest)
+        last[...] = newest
+        return chunks
 
     def link_out(c):
         return pltpu.make_async_copy(rec.at[c], srec.at[c], csem.at[c])
@@ -195,17 +202,17 @@
 
         lax.fori_loop(0, CAP // 8, body, jnp.zeros((rows, PTS), F32))
 
-    def prepare():
+    def prepare(part):
         lane8 = lax.broadcasted_iota(I32, (8, PTS), 0)
 
         def leaf(t, carry):
             sl = pl.ds(pl.multiple_of(t * PTS, PTS), PTS)
             raw = mb[0][t]
-            for d in range(3):
-                xb[t, d] = jnp.broadcast_to(raw[d:d + 1], (PTS, PTS)).T
             c = raw - 0.5
             cx, cy, cz = c[0:1], c[1:2], c[2:3]
             q = cx * cx + cy * cy + cz * cz
+            for d in range(3):
+                xb[t, d] = jnp.broadcast_to(raw[d:d + 1], (PTS, PTS)).T
 
             def stack(r0, r1, r2, r3, r4):
                 v = jnp.where(lane8 == 0, r0, 0.0)
@@ -221,7 +228,9 @@
             fy[:, sl] = jnp.concatenate([b1, b2, b1, b2, b3, b1], axis=0).astype(BF)
             return carry
 
-        lax.fori_loop(0, LEAF_DEV, leaf, 0)
+        lax.fori_loop(part * 8, part * 8 + 8, leaf, 0, unroll=2)
+
+    def prepare_counts():
         ids = near_ids_ref[...] - me * LEAF_DEV
         sub_i = lax.broadcasted_iota(I32, (LEAF_DEV, LEAF_DEV), 0)
         cnt = jnp.zeros((LEAF_DEV, LEAF_DEV), F32)
@@ -266,8 +275,7 @@
             kind, i = far_ready.pop(0)
             c = i + kind * RING
             if kind:
-                for sub in range(NSUB):
-                    pair_om(i, sub).wait_recv()
+                pair_om(i).wait_recv()
                 pair_pts(i).wait_recv()
             link_out(c).wait()
             far_chunk(c, (pbufs if kind else bufs)[i], (pmb if kind else mb)[i])
@@ -275,85 +283,77 @@
     for way in (0, 1):
         ring_pts(0, way).start()
         ring_om(0, 0, way).start()
-    make_table()
     for sub in range(1, NSUB):
         for way in (0, 1):
             ring_om(0, sub, way).start()
     pair_pts(0).start()
-    for sub in range(NSUB):
-        pair_om(0, sub).start()
+    pair_om(0).start()
+    make_table()
     last[...] = jnp.zeros((1, PTS), I32)
     chain[0] = jnp.zeros((rows, PTS), F32)
-    prepare()
     for way in (0, 1):
         ring_tab(0, way).start()
     pair_tab(0).start()
-    do_near(1)
-
-    def links(chunks):
-        for kind, i in chunks:
-            if kind:
-                pair_tab(i).wait_recv()
-            link(i + kind * RING, (ptb if kind else tb)[i])
-        return chunks
 
     for d in range(8):
         ways = [way for way in (0, 1) if small(d, way)]
-        for way in ways:
-            i = ends(d, way)[1]
-            ring_pts(d, way).wait_recv()
-            if d < 7 and small(d + 1, way):
-                ring_pts(d + 1, way).start()
-            for k in range(1, n_probe):
-                probe_pts(i, k).start()
-
-        def tables():
-            for way in ways:
-                i = ends(d, way)[1]
-                ring_tab(d, way).wait_recv()
-                if d < 7 and small(d + 1, way):
-                    ring_tab(d + 1, way).start()
-                pair_tab(i).start()
-
-        def points():
-            for way in ways:
-                i = ends(d, way)[1]
-                for k in range(1, n_probe):
-                    probe_pts_in(i, k).wait_recv()
-                pair_pts(i).start()
-
-        arrived = [(kind, ends(d, way)[1]) for kind in (0, 1) for way in ways]
+        blocks = [ends(d, way)[1] for way in ways]
+        arrived = [(kind, i) for kind in (0, 1) for i in blocks]
         if d == 0:
             arrived = [(1, 0)] + arrived
-        for sub in range(NSUB):
-            for way in (0, 1):
-                if sub not in subs(d, way):
-                    continue
+        if d < 7:
+            events = [[(0, sub), (1, sub)] for sub in range(NSUB)]
+        else:
+            events = [[(0, sub), (1, sub + NSUB // 2)] for sub in range(NSUB // 2)]
+        if d == 7:
+            do_far(1)
+        for e, event in enumerate(events):
+            if e == 0:
+                for way, i in zip(ways, blocks):
+                    ring_pts(d, way).wait_recv()
+                    if d < 7 and small(d + 1, way):
+                        ring_pts(d + 1, way).start()
+                    for k in range(1, n_probe):
+                        probe_pts(i, k).start()
+            for way, sub in event:
                 i = ends(d, way)[1]
                 ring_om(d, sub, way).wait_recv()
                 if d < 7 and sub in subs(d + 1, way):
                     ring_om(d + 1, sub, way).start()
-                pair_om(i, sub).start()
-            if sub == 0:
-                tables()
-            if d < 7:
-                do_near(2 if d == 0 else 1)
+            if e == len(events) - 1:
+                for i in blocks:
+                    pair_om(i).start()
+            if e == 0:
+                for way, i in zip(ways, blocks):
+                    ring_tab(d, way).wait_recv()
+                    if d < 7 and small(d + 1, way):
+                        ring_tab(d + 1, way).start()
+                    pair_tab(i).start()
+            if d == 0:
+                prepare(2 * e)
+                prepare(2 * e + 1)
+            elif d < 7:
+                do_near(2)
+                do_far(3 if d == 1 and e == 1 else 2)
+            else:
                 do_far(1)
-            if sub == 1:
-                points()
-        if d == 7:
-            links(arrived)
+            if e == len(events) - 1:
+                for i in blocks:
+                    for k in range(1, n_probe):
+                        probe_pts_in(i, k).wait_recv()
+                    pair_pts(i).start()
+        if d == 0:
+            prepare_counts()
+        links(arrived)
+        if d < 7:
+            do_near(2 if d == 0 else 1)
+        else:
             do_far(1)
-            for kind, i in arrived:
-                link_out(i + kind * RING).start()
-            do_far(len(far_ready))
-        else:
-            links(arrived)
-            do_near(1)
-            for kind, i in arrived:
-                link_out(i + kind * RING).start()
-            if d == 0:
-                prepare_merge()
+        for kind, i in arrived:
+            link_out(i + kind * RING).start()
+        if d == 0:
+            prepare_merge()
+        do_far(len(far_ready) if d == 7 else 0)
         far_ready += arrived
     last_out = pltpu.make_async_copy(last, slast, lsem)
     last_out.start()
@@ -388,8 +388,7 @@
     for cp in copies:
         cp.start()
     for i in range(RING):
-        for sub in range(NSUB):
-            pair_om(i, sub).wait_send()
+        pair_om(i).wait_send()
         pair_tab(i).wait_send()
         pair_pts(i).wait_send()
     for cp in copies:
@@ -423,7 +422,7 @@
             pltpu.VMEM((rows, n), BF),
             pltpu.VMEM((2 * RING, 1, PTS), I32),
             pltpu.VMEM((1, PTS), I32),
-            pltpu.VMEM((PTS, PTS), I32),
+            pltpu.VMEM((5, PTS, PTS), I32),
             pltpu.SMEM((2 * RING, 1, PTS), I32),
             pltpu.SMEM((1, PTS), I32),
             pltpu.VMEM((n, 48), BF),

time: 91.3 us -> 84.4 us (0.924)
  Pallas kernels: 87.5 us -> 80.7 us
    pallas_call x1, Pallas kernels: 87.5 us -> 80.7 us  [sample(): pl.pallas_call(kernel_body, out_shape=(jax.ShapeDtypeStruct((rows, n), F3...]
where the time goes in v1:
time: 84.4 us; the launch traced here: 84.3 us
  Pallas kernels  80.7 us (96%)
  local copies, waits for them, and re-layouts  2.94 us (3%)
    pallas_call x1, Pallas kernels, sample(): pl.pallas_call(kernel_body, out_shape=(jax.ShapeDtypeStruct((rows, n), F3...  80.7 us
    unnamed x4, local copies, waits for them, and re-layouts  2.94 us

profile of v1, /device:TPU:0, one launch (start us, length us, event | category | flops | bytes accessed | tf_op | source)
XLA Modules:
  0.0 84.3 jit_solution(11918691816147023802)
XLA Ops:
  0.6 80.7 %sample.1 = (f32[64,4096]{1,0:T(8,128)}, f32[64,256]{1,0:T(8,128)}) custom-call(bf16[64,4096]{1,0:T(8,128)(2,1)} %om_ref.1, f32[3,4096]{1,0:T(4,128)} %coords_ref.1, f32[1,4096]{1,0:T(1,128)} %bitcast.4, s32[24,32]{1,0:T(8,128)} %bitcast.5, s32[2,256]{1,0:T(2,128)} %far_pairs_ref.1, s32[32,32]{1,0:T(8,128)} %skel_ref.1, bf16[4,64,256]{2,1,0:T(8,128)(2,1)} %bitcast.3), custom_call_target="tpu_custom_call" | custom-call | tf_op jit(solution)/shard_map/sample/pallas_call | solution.py:410
  81.4 0.0 copy-start
  81.4 2.3 %copy.11 = f32[64,4096]{1,0:T(8,128)} copy(f32[64,4096]{1,0:T(8,128)} %get-tuple-element.4) | data formatting | bytes 2097152
  83.7 0.0 copy-done
  83.7 0.6 copy.12
Async XLA Ops:
  81.4 2.3 %copy-start = (f32[64,256]{1,0:T(8,128)S(1)}, f32[64,256]{1,0:T(8,128)}, u32[]{:S(2)}) copy-start(f32[64,256]{1,0:T(8,128)} %get-tuple-element.5) | copy-start | bytes 196612
